TPU v7x, 32 devices: a whole 2x2x4 slice. The times are simulated.
32 devices in a mesh: scen: 2 (over x), tm: 16 (over z, y, core).
Axes of the slice: x: 2, y: 2, z: 4, core: 2. Of those that a mesh axis runs over, the one named last changes fastest.
Arguments:
- base_injection: bfloat16 [32, 36864], P(('scen', 'tm')), parts along dimension 0, may hold values from -6 to 6
- ptdf_tiles: bfloat16 [128, 80, 128, 128], P(None, 'tm'), may hold values from -0.0625 to 0.0625
- tile_block: int32 [128, 80], P(None, 'tm'), may hold values from 0 to 17
- limits: float32 [16384], replicated, may hold values from 0.5 to 2
- stor_bus: int32 [2048], replicated, may hold values from 0 to 36863
- stor_gain: float32 [2048], replicated, may hold values from 0.5 to 4
- soc_init: float32 [32, 2048], P(('scen', 'tm')), parts along dimension 0, may hold values from 0 to 1
Outputs:
- injection: float32 [32, 36864], P(('scen', 'tm')), parts along dimension 0
- line_dual: float32 [32, 16384], P(('scen', 'tm')), parts along dimension 0
- level: float32 [32, 2048], P(('scen', 'tm')), parts along dimension 0
There are 2 independent parts, one for each index of `scen`. A program takes and returns all parts, laid end to end along the dimension named above; an argument that names none is the same for every part. Nothing has to cross between parts.
All inputs are finite; a program needn't handle non-finite values.
Results may differ from a plain program's by a relative error of at most 0.012.
The roundings to bfloat16 on the way count: a program that leaves them out, or rounds other values in their place, can miss the bound.
Values may be sent and summed in bfloat16 or wider, within the bound.
A program may use at most 128 MiB of HBM per device.

v0:
```python
import functools

import jax
import jax.numpy as jnp
from jax import lax
from jax.experimental import pallas as pl
from jax.experimental.pallas import tpu as pltpu
from jax.sharding import PartitionSpec as P

ITERS = 2
STREAMS = 4

step_size = 0.5
penalty = 4.0
ramp_weight = 0.5

VM = pl.BlockSpec(memory_space=pltpu.VMEM)
MESH = pl.DeviceIdType.MESH


def peer(index):
    return {"tm": index}


def greet(others):
    barrier = pltpu.get_barrier_semaphore()
    for other in others:
        pl.semaphore_signal(barrier, inc=1, device_id=peer(other), device_id_type=MESH)
    pl.semaphore_wait(barrier, len(others))


def opening_kernel(n, base_ref, out_ref, rows, wide, send_sem, recv_sem):
    me = lax.axis_index("tm")
    reach = rows.shape[2]
    blocks, _, width = out_ref.shape
    others = [lax.rem(me + k, n) for k in range(1, n)]
    greet(others)
    copies = []
    for k, other in enumerate(others):
        copy = pltpu.make_async_remote_copy(
            src_ref=base_ref.at[:, pl.ds(pl.multiple_of(other * reach, reach), reach)],
            dst_ref=rows.at[me],
            send_sem=send_sem.at[k],
            recv_sem=recv_sem.at[k],
            device_id=peer(other),
            device_id_type=MESH,
        )
        copy.start()
        copies.append(copy)
    rows[me] = base_ref[:, pl.ds(pl.multiple_of(me * reach, reach), reach)]
    for copy in copies:
        copy.wait()
    for h in range(n):
        row = rows[h].astype(jnp.float32)
        for b in range(blocks):
            wide[b, h:h + 1, :] = row[:, b * width:(b + 1) * width]
    out_ref[...] = wide[...].astype(out_ref.dtype)


def opening(n, base, width):
    reach = base.shape[1] // n
    shape = (reach // width, n, width)
    return pl.pallas_call(
        functools.partial(opening_kernel, n),
        out_shape=jax.ShapeDtypeStruct(shape, base.dtype),
        in_specs=[VM],
        out_specs=VM,
        scratch_shapes=[
            pltpu.VMEM((n, 1, reach), base.dtype),
            pltpu.VMEM(shape, jnp.float32),
            pltpu.SemaphoreType.DMA((n - 1,)),
            pltpu.SemaphoreType.DMA((n - 1,)),
        ],
        compiler_params=pltpu.CompilerParams(collective_id=0, has_side_effects=True),
        name="opening",
    )(base)


def closing_kernel(
    n, inj_ref, dual_ref, level_ref, inj_out, dual_out, level_out,
    dual_rows, level_rows, level_recv, send_sem, recv_sem,
):
    me = lax.axis_index("tm")
    reach = inj_ref.shape[2]
    span = dual_rows.shape[2]
    width = dual_ref.shape[1]
    hours = dual_rows.shape[0]
    for h in range(hours):
        for g in range(span // width):
            dual_rows[h, :, g * width:(g + 1) * width] = dual_ref[g * hours + h:g * hours + h + 1, :]
    level_rows[...] = level_ref[...].astype(level_rows.dtype)
    others = [lax.rem(me + k, n) for k in range(1, n)]
    greet(others)
    inj_here = inj_out.at[:, pl.ds(pl.multiple_of(me * reach, reach), reach)]
    dual_here = dual_out.at[:, pl.ds(pl.multiple_of(me * span, span), span)]
    copies = []
    for k, other in enumerate(others):
        for part, (src, dst) in enumerate((
            (inj_ref.at[other], inj_here),
            (dual_rows.at[other], dual_here),
            (level_rows.at[other], level_recv.at[k]),
        )):
            copy = pltpu.make_async_remote_copy(
                src_ref=src, dst_ref=dst,
                send_sem=send_sem.at[part, k], recv_sem=recv_sem.at[part, k],
                device_id=peer(other), device_id_type=MESH,
            )
            copy.start()
            copies.append(copy)
    inj_here[...] = inj_ref[me]
    dual_here[...] = dual_rows[me]
    for copy in copies:
        copy.wait()
    level = level_ref[me]
    for k in range(n - 1):
        level = level + level_recv[k].astype(jnp.float32)
    for q in range(level.shape[0]):
        level_out[:, q * width:(q + 1) * width] = level[q:q + 1]


def closing(n, inj, dual, level, collective_id):
    hours, _, reach = inj.shape
    rows, width = dual.shape
    span = rows // hours * width
    return pl.pallas_call(
        functools.partial(closing_kernel, n),
        out_shape=(
            jax.ShapeDtypeStruct((1, n * reach), jnp.float32),
            jax.ShapeDtypeStruct((1, n * span), jnp.float32),
            jax.ShapeDtypeStruct((1, level.shape[1] * level.shape[2]), jnp.float32),
        ),
        in_specs=[VM] * 3,
        out_specs=(VM, VM, VM),
        scratch_shapes=[
            pltpu.VMEM((hours, 1, span), jnp.float32),
            pltpu.VMEM(level.shape, jnp.bfloat16),
            pltpu.VMEM((n - 1,) + level.shape[1:], jnp.bfloat16),
            pltpu.SemaphoreType.DMA((3, n - 1)),
            pltpu.SemaphoreType.DMA((3, n - 1)),
        ],
        compiler_params=pltpu.CompilerParams(collective_id=collective_id, has_side_effects=True),
        name="closing",
    )(inj, dual, level)


def flow_clip_kernel(
    n, hours, opens, block_ref, sent_ref, extra_ref, limits_ref, tiles_ref, all_ref, own_ref, *refs
):
    if opens:
        level_ref, *refs = refs
        *refs, level_recv, level_send_sem, level_recv_sem = refs
    (
        held, theirs, mine, first_recv, first_sum, second_recv,
        tile_sem, pair_send, pair_recv, row_send, row_recv,
        far_send, far_recv, mid_send, mid_recv, near_send, near_recv,
    ) = refs
    half, quarter = n // 2, n // 4
    me = lax.axis_index("tm")
    core = lax.rem(me, 2)
    spot = me // 2
    partner = me + 1 - 2 * core
    slots, own_groups, depth = held.shape[:3]
    spots = [lax.rem(spot + k, half) for k in range(1, half)]

    def remote(src, dst, send, recv, device):
        return pltpu.make_async_remote_copy(
            src_ref=src, dst_ref=dst, send_sem=send, recv_sem=recv,
            device_id=peer(device), device_id_type=MESH,
        )

    def owner(k, other):
        return lax.rem(spot + k + 1, half) * 2 + (1 - core if other else core)

    def fetch(k, other, slot):
        return pltpu.make_async_copy(
            tiles_ref.at[pl.ds(owner(k, other) * own_groups, own_groups)], held.at[slot], tile_sem.at[slot]
        )

    def product(k, other, slot, out):
        first = owner(k, other) * own_groups
        for g in range(own_groups):
            picked = jnp.concatenate([sent_ref[block_ref[first + g, t]] for t in range(depth)], axis=1)
            wide = jnp.concatenate([held[slot, g, t] for t in range(depth)], axis=1)
            out[k, g * hours:(g + 1) * hours] = lax.dot_general(
                picked, wide, (((1,), (1,)), ((), ())), preferred_element_type=jnp.float32
            )

    def pair(k):
        return remote(theirs.at[k], first_recv.at[k], pair_send.at[k], pair_recv.at[k], partner)

    def row(k):
        return remote(
            first_sum.at[k], second_recv.at[k], row_send.at[k], row_recv.at[k],
            lax.rem(spot + k + 1, half) * 2 + core,
        )

    ahead = slots // 2
    for k in range(ahead):
        fetch(k, True, 2 * k).start()
        fetch(k, False, 2 * k + 1).start()
    levels = []
    if opens:
        everyone = [lax.rem(me + k, n) for k in range(1, n)]
        greet(everyone)
        for k, other in enumerate(everyone):
            copy = remote(extra_ref, level_recv.at[me], level_send_sem.at[k], level_recv_sem.at[k], other)
            copy.start()
            levels.append(copy)
        level_recv[me] = extra_ref[...]
    else:
        greet([partner] + [s * 2 + core for s in spots])

    def pass_on(k):
        pair(k).wait_recv()
        first_sum[k] = (mine[k] + first_recv[k]).astype(jnp.bfloat16)
        row(k).start()

    def step(k, carry):
        slot = lax.rem(k, ahead) * 2
        for other, out in ((True, theirs), (False, mine)):
            place = slot if other else slot + 1
            fetch(k, other, place).wait()
            product(k, other, place, out)
            if other:
                pair(k).start()

            @pl.when(k + ahead < half)
            def _():
                fetch(k + ahead, other, place).start()

        @pl.when(k >= 1)
        def _():
            pass_on(k - 1)

        return carry

    lax.fori_loop(0, half, step, 0)
    pair(half - 1).wait_recv()
    total = mine[half - 1] + first_recv[half - 1]
    for k in range(half - 1):
        row(k).wait_recv()
        total = total + second_recv[k].astype(jnp.float32)
    rows = total.shape[0]
    if not opens:
        total = total + extra_ref[...]
    shifted = total.reshape(rows // hours, hours, total.shape[1])
    bound = limits_ref[pl.ds(me * own_groups, own_groups), :][:, None, :]
    clipped = jnp.minimum(jnp.maximum(shifted, -bound), bound)
    dual = (shifted - clipped).reshape(total.shape)
    own_ref[...] = dual
    all_ref[me] = dual.astype(jnp.bfloat16)

    far, lane = me // 4, lax.rem(me, 4)
    across = me + 2 - 4 * lax.rem(me // 2, 2)
    copies = []

    def send(chunk, sends, recvs, k, device):
        copy = remote(all_ref.at[chunk], all_ref.at[chunk], sends.at[k], recvs.at[k], device)
        copy.start()
        copies.append(copy)
        return copy

    fars = [
        send(me, far_send, far_recv, k, lax.rem(far + k + 1, quarter) * 4 + lane) for k in range(quarter - 1)
    ]
    mids = [send(me, mid_send, mid_recv, 0, across)]
    send(me, near_send, near_recv, 0, partner)
    for k in range(quarter - 1):
        fars[k].wait_recv()
        source = lax.rem(far + quarter - k - 1, quarter) * 4
        mids.append(send(source + lane, mid_send, mid_recv, k + 1, across))
        send(source + lane, near_send, near_recv, k + 1, partner)
    nears = copies[quarter:quarter + 1] + copies[quarter + 2::2]
    for k in range(quarter):
        mids[k].wait_recv()
        source = lax.rem(far + quarter - k, quarter) * 4 + lax.rem(across, 4)
        nears.append(send(source, near_send, near_recv, quarter + k, partner))
    if opens:
        for copy in levels:
            copy.wait()
        for h in range(n):
            level_ref[h:h + 1, :] = level_recv[h]
    for copy in nears:
        copy.wait_recv()
    for copy in copies:
        copy.wait_send()
    for k in range(half):
        pair(k).wait_send()
    for k in range(half - 1):
        row(k).wait_send()


def flow_clip(n, tile_block, sent, extra, limits, tiles, opens, collective_id):
    half, quarter = n // 2, n // 4
    hours = sent.shape[1]
    own_groups = tiles.shape[0] // n
    chunk = (own_groups * hours, tiles.shape[2])
    slots = 4
    dma = pltpu.SemaphoreType.DMA
    outs = [
        jax.ShapeDtypeStruct((n,) + chunk, jnp.bfloat16),
        jax.ShapeDtypeStruct(chunk, jnp.float32),
    ]
    more = []
    if opens:
        outs.append(jax.ShapeDtypeStruct((n, extra.shape[1]), extra.dtype))
        more = [pltpu.VMEM((n,) + extra.shape, extra.dtype), dma((n - 1,)), dma((n - 1,))]
    return pl.pallas_call(
        functools.partial(flow_clip_kernel, n, hours, opens),
        out_shape=tuple(outs),
        in_specs=[pl.BlockSpec(memory_space=pltpu.SMEM)] + [VM] * 3 + [pl.BlockSpec(memory_space=pl.ANY)],
        out_specs=(VM,) * len(outs),
        scratch_shapes=[
            pltpu.VMEM((slots, own_groups) + tiles.shape[1:], tiles.dtype),
            pltpu.VMEM((half,) + chunk, jnp.float32),
            pltpu.VMEM((half,) + chunk, jnp.float32),
            pltpu.VMEM((half,) + chunk, jnp.float32),
            pltpu.VMEM((half - 1,) + chunk, jnp.bfloat16),
            pltpu.VMEM((half - 1,) + chunk, jnp.bfloat16),
            dma((slots,)),
            dma((half,)), dma((half,)),
            dma((half - 1,)), dma((half - 1,)),
            dma((quarter - 1,)), dma((quarter - 1,)),
            dma((quarter,)), dma((quarter,)),
            dma((half,)), dma((half,)),
        ] + more,
        compiler_params=pltpu.CompilerParams(collective_id=collective_id, has_side_effects=True),
        name=f"flow_clip_{collective_id}",
    )(tile_block, sent, extra, limits, tiles)


def tile_specs(tiles, count):
    shape = (count // STREAMS,) + tiles.shape[1:]
    return [
        pl.BlockSpec(shape, lambda i, b, part=part: (i * STREAMS + part, 0, 0, 0))
        for part in range(STREAMS)
    ]


def price_kernel(
    unit_chunk, last, depth, block_ref, dual_ref, *refs
):
    step = pl.program_id(0)
    tile_refs, refs = refs[:STREAMS], refs[STREAMS:]
    base_ref, inj_ref, level_ref, gain_ref, unit_ref, new_inj_ref, second_ref, new_level_ref = refs[:-depth]
    totals = refs[-depth:]
    each = tile_refs[0].shape[0]
    count = each * STREAMS

    @pl.when(step == 0)
    def _():
        for total in totals:
            total[...] = jnp.zeros_like(total)

    for g in range(count):
        wide = jnp.concatenate([tile_refs[g // each][g % each, k] for k in range(depth)], axis=1)
        part = jnp.dot(dual_ref[g], wide, preferred_element_type=jnp.float32)
        width = part.shape[1] // depth
        for k in range(depth):
            at = block_ref[step * count + g, k]
            totals[k][at] += part[:, k * width:(k + 1) * width]

    @pl.when(step == pl.num_programs(0) - 1)
    def _():
        price = totals[0][...]
        for total in totals[1:]:
            price = price + total[...]
        blocks, hours, width = price.shape
        units = level_ref.shape[1]
        flat = price.astype(jnp.bfloat16).reshape(blocks * hours, width)
        moved = jnp.zeros((blocks * hours, width), jnp.float32)
        for start in range(0, units, unit_chunk):
            span = pl.ds(start, unit_chunk)
            bus = unit_ref[:, span]
            first = lax.axis_index("tm") * blocks
            block = jnp.broadcast_to(lax.div(bus, width) - first, (hours, unit_chunk))
            lane = lax.rem(bus, width)
            rows = lax.broadcasted_iota(jnp.int32, (width, unit_chunk), 0)
            chosen = jnp.where(rows == lane, 1.0, 0.0).astype(jnp.bfloat16)
            level = level_ref[:, span]
            before = pltpu.roll(level, 1, 0)
            charge = level - before
            spread = jnp.concatenate(
                [jnp.where(block == r, charge, 0.0).astype(jnp.bfloat16) for r in range(blocks)], axis=0
            )
            moved = moved + lax.dot_general(
                spread, chosen, (((1,), (1,)), ((), ())), preferred_element_type=jnp.float32
            )
            found = jnp.dot(flat, chosen, preferred_element_type=jnp.float32)
            store_price = jnp.zeros_like(level)
            for r in range(blocks):
                store_price = store_price + jnp.where(block == r, found[r * hours:(r + 1) * hours], 0.0)
            new_level = 0.5 * (level + before) - gain_ref[:, span] * store_price
            if last:
                new_level = jnp.where((block >= 0) & (block < blocks), new_level, 0.0)
                for q in range(unit_chunk // width):
                    new_level_ref[:, start // width + q, :] = new_level[:, q * width:(q + 1) * width]
            else:
                new_level_ref[:, span] = new_level
        for r in range(blocks):
            inj = inj_ref[r].astype(jnp.float32)
            ramp = 2.0 * inj - pltpu.roll(inj, 1, 0) - pltpu.roll(inj, hours - 1, 0)
            updated = inj - step_size * (
                (inj - base_ref[r].astype(jnp.float32)) + penalty * price[r] + ramp_weight * ramp
            )
            updated = updated - step_size * moved[r * hours:(r + 1) * hours]
            if last:
                for h in range(hours):
                    new_inj_ref[h, :, r * width:(r + 1) * width] = updated[h:h + 1]
            else:
                new_inj_ref[r] = updated
                second_ref[r] = updated.astype(jnp.bfloat16)
        if last:
            second_ref[...] = jnp.zeros_like(second_ref)


def price_update(last, tile_block, dual_all, tiles, base, inj, level, gain, unit_bus, count):
    groups, depth, lines, width = tiles.shape
    blocks, hours = base.shape[:2]
    units = level.shape[1]
    chunk = 512 if units % 512 == 0 else units
    whole3 = pl.BlockSpec((blocks, hours, width), lambda i, b: (0, 0, 0))
    whole2 = pl.BlockSpec((hours, units), lambda i, b: (0, 0))
    line2 = pl.BlockSpec((1, units), lambda i, b: (0, 0))
    if last:
        outs = (
            ((hours, 1, blocks * width), jnp.float32),
            ((8, 128), jnp.float32),
            ((hours, units // width, width), jnp.float32),
        )
    else:
        outs = ((base.shape, jnp.float32), (base.shape, jnp.bfloat16), (level.shape, jnp.float32))
    return pl.pallas_call(
        functools.partial(price_kernel, chunk, last, depth),
        out_shape=tuple(jax.ShapeDtypeStruct(*out) for out in outs),
        grid_spec=pltpu.PrefetchScalarGridSpec(
            num_scalar_prefetch=1,
            grid=(groups // count,),
            in_specs=[
                pl.BlockSpec((count, hours, lines), lambda i, b: (i, 0, 0)),
                *tile_specs(tiles, count),
                whole3, whole3, whole2, line2, line2,
            ],
            out_specs=tuple(
                pl.BlockSpec(shape, lambda i, b, rank=len(shape): (0,) * rank) for shape, _ in outs
            ),
            scratch_shapes=[pltpu.VMEM(base.shape, jnp.float32)] * depth,
        ),
        name="price",
    )(tile_block, dual_all, *([tiles] * STREAMS), base, inj, level, gain, unit_bus)


def shards(base_injection, ptdf_tiles, tile_block, limits, stor_bus, stor_gain, soc_init):
    n = lax.axis_size("tm")
    hours = n * base_injection.shape[0]
    groups, _, lines, width = ptdf_tiles.shape
    units = soc_init.shape[1]
    count = 32

    base = opening(n, base_injection, width)
    unit_bus = stor_bus.reshape(1, units)
    gain = stor_gain.reshape(1, units)
    bounds = limits.reshape(groups, lines)

    inj, sent = base, base
    for iteration in range(ITERS):
        opens = iteration == 0
        dual_all, dual, *gathered = flow_clip(
            n, tile_block, sent, soc_init if opens else dual, bounds, ptdf_tiles, opens, 1 + iteration
        )
        if opens:
            level, = gathered
        inj, sent, level = price_update(
            iteration == ITERS - 1, tile_block, dual_all.reshape(groups, hours, lines), ptdf_tiles,
            base, inj, level, gain, unit_bus, count,
        )
    return closing(n, inj, dual, level, 1 + ITERS)


def solution(mesh):
    in_specs = (
        P(("scen", "tm"), None),
        P(None, "tm", None, None),
        P(None, "tm"),
        P(),
        P(),
        P(),
        P(("scen", "tm"), None),
    )
    out_specs = (P(("scen", "tm"), None), P(("scen", "tm"), None), P(("scen", "tm"), None))
    return jax.shard_map(shards, mesh=mesh, in_specs=in_specs, out_specs=out_specs, check_vma=False)
```

profile of v0, /device:TPU:0, one launch (start us, length us, event | category | flops | bytes accessed | tf_op | source)
XLA Modules:
  0.0 109.9 jit_solution(17550420949109246808)
XLA Ops:
  0.6 1.4 %copy.13.block_ref = s32[128,5]{1,0:T(8,128)} copy(s32[128,5]{0,1:T(8,128)} %param.9) | data formatting | bytes 5120 | tf_op args[2]
  2.1 11.0 %opening.1.sent_ref.refs_4_.refs_5_ = bf16[18,16,128]{2,1,0:T(8,128)(2,1)} custom-call(bf16[1,36864]{1,0:T(2,128)(2,1)} %base_ref.1), custom_call_target="tpu_custom_call" | custom-call | tf_op jit(solution)/shard_map/opening/pallas_call | solution.py:63
  13.0 29.7 %flow_clip_1.1 = (bf16[16,128,128]{2,1,0:T(8,128)(2,1)}, f32[128,128]{1,0:T(8,128)}, f32[16,2048]{1,0:T(8,128)}) custom-call(s32[128,5]{1,0:T(8,128)} %copy.13.block_ref, bf16[18,16,128]{2,1,0:T(8,128)(2,1)} %opening.1.sent_ref.refs_4_.refs_5_, f32[1,2048]{1,0:T(1,128)} %extra_ref.1, f32[128,128]{1,0:T(8,128)} %bitcast.7, bf16[128,5,128,128]{3,2,1,0:T(8,128)(2,1)} %refs_3_.3), custom_call_target="tpu_custom_call" | custom-call | tf_op jit(solution)/shard_map/flow_clip_1/pallas_call | solution.py:308
  42.8 13.6 %price.2 = (f32[18,16,128]{2,1,0:T(8,128)}, bf16[18,16,128]{2,1,0:T(8,128)(2,1)}, f32[16,2048]{1,0:T(8,128)}) custom-call(s32[128,5]{1,0:T(8,128)} %copy.13.block_ref, bf16[128,16,128]{2,1,0:T(8,128)(2,1)} %bitcast.6, bf16[128,5,128,128]{3,2,1,0:T(8,128)(2,1)} %refs_3_.3, bf16[128,5,128,128]{3,2,1,0:T(8,128)(2,1)} %refs_3_.3, ...), custom_call_target="tpu_custom_call" | custom-call | tf_op jit(solution)/shard_map/price/pallas_call | solution.py:433
  56.4 25.9 %flow_clip_2.1 = (bf16[16,128,128]{2,1,0:T(8,128)(2,1)}, f32[128,128]{1,0:T(8,128)}) custom-call(s32[128,5]{1,0:T(8,128)} %copy.13.block_ref, bf16[18,16,128]{2,1,0:T(8,128)(2,1)} %get-tuple-element.15.sent_ref, f32[128,128]{1,0:T(8,128)} %get-tuple-element.16.extra_ref, f32[128,128]{1,0:T(8,128)} %bitcast.8, bf16[128,5,128,128]{3,2,1,0:T(8,128)(2,1)} %refs_3_.3), custom_call_target="tpu_custom_call" | custom-call | tf_op jit(solution)/shard_map/flow_clip_2/pallas_call | solution.py:308
  82.3 13.0 %price.3 = (f32[16,1,2304]{2,1,0:T(1,128)}, f32[8,128]{1,0:T(8,128)}, f32[16,16,128]{2,1,0:T(8,128)}) custom-call(s32[128,5]{1,0:T(8,128)} %copy.13.block_ref, bf16[128,16,128]{2,1,0:T(8,128)(2,1)} %bitcast.5, bf16[128,5,128,128]{3,2,1,0:T(8,128)(2,1)} %refs_3_.3, bf16[128,5,128,128]{3,2,1,0:T(8,128)(2,1)} %refs_3_.3, bf16[128,5,128,128]{3,2,1,0:T(8,128)(2,1)} %refs_3_.3, ...), custom_call_target="tpu_custom_call" | custom-call | tf_op jit(solution)/shard_map/price/pallas_call | solution.py:433
  95.3 10.2 %closing.1 = (f32[1,36864]{1,0:T(1,128)}, f32[1,16384]{1,0:T(1,128)}, f32[1,2048]{1,0:T(1,128)}) custom-call(f32[16,1,2304]{2,1,0:T(1,128)} %get-tuple-element.20.inj_ref, f32[128,128]{1,0:T(8,128)} %get-tuple-element.21.dual_ref, f32[16,16,128]{2,1,0:T(8,128)} %get-tuple-element.22.level_ref), custom_call_target="tpu_custom_call" | custom-call | tf_op jit(solution)/shard_map/closing/pallas_call | solution.py:125
  105.5 1.6 %copy.17 = f32[1,36864]{1,0:T(1,128)} copy(f32[1,36864]{1,0:T(1,128)} %get-tuple-element.26) | data formatting | bytes 294912
  107.1 1.5 %copy.18 = f32[1,16384]{1,0:T(1,128)} copy(f32[1,16384]{1,0:T(1,128)} %get-tuple-element.27) | data formatting | bytes 131072
  108.6 1.3 %copy.19 = f32[1,2048]{1,0:T(1,128)} copy(f32[1,2048]{1,0:T(1,128)} %get-tuple-element.28) | data formatting | bytes 16384
where the time goes:
time: 111 us; the launch traced here: 110 us
  Pallas kernels  103 us (93%)
  local copies, waits for them, and re-layouts  5.77 us (5%)
    pallas_call x2, Pallas kernels, flow_clip(): pl.pallas_call(functools.partial(flow_clip_kernel, n, hours, opens), out_...  55.7 us
    pallas_call x2, Pallas kernels, price_update(): pl.pallas_call(functools.partial(price_kernel, chunk, last, depth), out_s...  26.5 us
    pallas_call x1, Pallas kernels, opening(): pl.pallas_call(functools.partial(opening_kernel, n), out_shape=jax.ShapeD...  11 us
    pallas_call x1, Pallas kernels, closing(): pl.pallas_call(functools.partial(closing_kernel, n), out_shape=(jax.Shape...  10.2 us
    unnamed x4, local copies, waits for them, and re-layouts  5.77 us

commit v1 on v0

v1 whole, which is shorter than its diff:
```python
import functools

import jax
import jax.numpy as jnp
from jax import lax
from jax.experimental import pallas as pl
from jax.experimental.pallas import tpu as pltpu
from jax.sharding import PartitionSpec as P

ITERS = 2

step_size = 0.5
penalty = 4.0
ramp_weight = 0.5

VM = pl.BlockSpec(memory_space=pltpu.VMEM)
MESH = pl.DeviceIdType.MESH


def admm_kernel(
    n, unit_chunk, block_ref, block_rows_ref, base_row_ref, limits_ref, bus_ref, gain_ref, soc_ref, tiles_ref,
    inj_out, dual_out, level_out,
    held, rows, base, inj, sent, price, level_recv, level, pointers, table,
    theirs, mine, first_recv, first_sum, second_recv, own, all_dual, slots,
    inj_rows, dual_rows, level_rows, level_parts, level_last,
    tile_sem, table_sem, start_send, start_recv, pair_send, pair_recv, row_send, row_recv,
    far_send, far_recv, mid_send, mid_recv, near_send, near_recv, end_send, end_recv,
):
    half, quarter = n // 2, n // 4
    groups, depth, _, width = held.shape
    blocks, hours = base.shape[:2]
    reach = blocks * width
    own_groups = groups // n
    span = own_groups * width
    units = level.shape[1]
    me = lax.axis_index("tm")
    core = lax.rem(me, 2)
    side = lax.rem(me // 2, 2)
    spot = me // 2
    far, lane = me // 4, lax.rem(me, 4)
    partner = me + 1 - 2 * core
    across = me + 2 - 4 * side
    everyone = [lax.rem(me + k, n) for k in range(1, n)]

    def remote(src, dst, send, recv, device):
        return pltpu.make_async_remote_copy(
            src_ref=src, dst_ref=dst, send_sem=send, recv_sem=recv,
            device_id={"tm": device}, device_id_type=MESH,
        )

    def owner(k, other):
        return lax.rem(spot + k + 1, half) * 2 + (1 - core if other else core)

    def fetch(k, other):
        place = pl.ds(owner(k, other) * own_groups, own_groups)
        return pltpu.make_async_copy(
            tiles_ref.at[place], held.at[place], tile_sem.at[2 * k + (0 if other else 1)]
        )

    def chunk_at(pos):
        z = lax.rem(far + quarter - lax.rem(pos, quarter), quarter)
        y = lax.rem(side + lax.rem(pos // quarter, 2), 2)
        c = lax.rem(core + pos // half, 2)
        return z * 4 + y * 2 + c

    for k in range(half):
        fetch(k, True).start()
        fetch(k, False).start()

    barrier = pltpu.get_barrier_semaphore()
    for other in everyone:
        pl.semaphore_signal(barrier, inc=1, device_id={"tm": other}, device_id_type=MESH)

    group_pos = []
    for dim in (0, 1):
        g = lax.broadcasted_iota(jnp.int32, (groups, groups), dim)
        dev = lax.div(g, own_groups)
        turn = lax.rem(far + quarter - lax.div(dev, 4), quarter)
        other_side = lax.rem(lax.rem(lax.div(dev, 2), 2) + side, 2)
        other_core = lax.rem(lax.rem(dev, 2) + core, 2)
        pos = (other_core * half + other_side * quarter + turn) * own_groups + lax.rem(g, own_groups)
        group_pos.append(pos)
    down, along = group_pos
    numbers = lax.broadcasted_iota(jnp.int32, (groups, groups), 1)
    for k in range(depth):
        here = jnp.broadcast_to(block_rows_ref[k:k + 1, :], (groups, groups))
        there = here.T
        before = jnp.where((here == there) & (down < along), down + 1, 0)
        pointers[k:k + 1, :] = jnp.max(before, axis=0, keepdims=True)
        final = jnp.where(there == numbers, down + 1, 0)
        pointers[depth + k:depth + k + 1, :] = jnp.max(final, axis=0, keepdims=True)
    to_table = pltpu.make_async_copy(pointers, table, table_sem.at[0])
    to_table.start()
    own[...] = jnp.zeros_like(own)
    for k in range(depth):
        slots[k, 0] = jnp.zeros((hours, width), jnp.float32)

    pl.semaphore_wait(barrier, n - 1)

    starts = []
    for k, other in enumerate(everyone):
        copy = remote(
            base_row_ref.at[:, pl.ds(pl.multiple_of(other * reach, reach), reach)], rows.at[me],
            start_send.at[0, k], start_recv.at[0, k], other,
        )
        copy.start()
        starts.append(copy)
    levels = []
    for k, other in enumerate(everyone):
        copy = remote(soc_ref, level_recv.at[me], start_send.at[1, k], start_recv.at[1, k], other)
        copy.start()
        levels.append(copy)
    rows[me] = base_row_ref[:, pl.ds(pl.multiple_of(me * reach, reach), reach)]
    level_recv[me] = soc_ref[...]
    to_table.wait()
    for copy in starts:
        copy.wait()
    for h in range(n):
        row = rows[h].astype(jnp.float32)
        for b in range(blocks):
            base[b, h:h + 1, :] = row[:, b * width:(b + 1) * width]
    inj[...] = base[...]
    sent[...] = base[...].astype(sent.dtype)

    def product(it, k, other, out):
        first = owner(k, other) * own_groups
        for g in range(own_groups):
            picked = jnp.concatenate([sent[block_ref[t, first + g]] for t in range(depth)], axis=1)
            wide = jnp.concatenate([held[first + g, t] for t in range(depth)], axis=1)
            out[it, k, g * hours:(g + 1) * hours] = lax.dot_general(
                picked, wide, (((1,), (1,)), ((), ())), preferred_element_type=jnp.float32
            )

    def pair(it, k):
        return remote(
            theirs.at[it, k], first_recv.at[it, k], pair_send.at[it, k], pair_recv.at[it, k], partner
        )

    def row(it, k):
        return remote(
            first_sum.at[it, k], second_recv.at[it, k], row_send.at[it, k], row_recv.at[it, k],
            lax.rem(spot + k + 1, half) * 2 + core,
        )

    def far_copy(it, k):
        chunk = all_dual.at[it, me]
        device = lax.rem(far + k + 1, quarter) * 4 + lane
        return remote(chunk, chunk, far_send.at[it, k], far_recv.at[it, k], device)

    def mid_copy(it, k):
        chunk = all_dual.at[it, chunk_at(k)]
        return remote(chunk, chunk, mid_send.at[it, k], mid_recv.at[it, k], across)

    def near_copy(it, k):
        chunk = all_dual.at[it, chunk_at(k)]
        return remote(chunk, chunk, near_send.at[it, k], near_recv.at[it, k], partner)

    def pass_on(it, k):
        pair(it, k).wait_recv()
        first_sum[it, k] = (mine[it, k] + first_recv[it, k]).astype(jnp.bfloat16)
        row(it, k).start()

    def add_price(it, pos):
        chunk = chunk_at(pos)
        for g in range(own_groups):
            group = chunk * own_groups + g
            place = pos * own_groups + g + 1
            wide = jnp.concatenate([held[group, k] for k in range(depth)], axis=1)
            part = jnp.dot(
                all_dual[it, chunk, g * hours:(g + 1) * hours], wide, preferred_element_type=jnp.float32
            )
            for k in range(depth):
                slots[k, place] = slots[k, table[k, group]] + part[:, k * width:(k + 1) * width]

    def loop(count, body):
        def step(k, carry):
            body(k)
            return carry

        lax.fori_loop(0, count, step, 0)

    def update():
        for r in range(blocks):
            total = slots[0, table[depth, r]]
            for k in range(1, depth):
                total = total + slots[k, table[depth + k, r]]
            price[r] = total
        flat = price[...].astype(jnp.bfloat16).reshape(blocks * hours, width)
        moved = jnp.zeros((blocks * hours, width), jnp.float32)
        for start in range(0, units, unit_chunk):
            part = pl.ds(start, unit_chunk)
            bus = bus_ref[:, part]
            block = jnp.broadcast_to(lax.div(bus, width) - me * blocks, (hours, unit_chunk))
            spots = lax.broadcasted_iota(jnp.int32, (width, unit_chunk), 0)
            chosen = jnp.where(spots == lax.rem(bus, width), 1.0, 0.0).astype(jnp.bfloat16)
            now = level[:, part]
            before = pltpu.roll(now, 1, 0)
            charge = now - before
            spread = jnp.concatenate(
                [jnp.where(block == r, charge, 0.0).astype(jnp.bfloat16) for r in range(blocks)], axis=0
            )
            moved = moved + lax.dot_general(
                spread, chosen, (((1,), (1,)), ((), ())), preferred_element_type=jnp.float32
            )
            found = jnp.dot(flat, chosen, preferred_element_type=jnp.float32)
            store_price = jnp.zeros_like(now)
            for r in range(blocks):
                store_price = store_price + jnp.where(block == r, found[r * hours:(r + 1) * hours], 0.0)
            level[:, part] = 0.5 * (now + before) - gain_ref[:, part] * store_price
        for r in range(blocks):
            now = inj[r]
            ramp = 2.0 * now - pltpu.roll(now, 1, 0) - pltpu.roll(now, hours - 1, 0)
            updated = now - step_size * ((now - base[r]) + penalty * price[r] + ramp_weight * ramp)
            updated = updated - step_size * moved[r * hours:(r + 1) * hours]
            inj[r] = updated
            sent[r] = updated.astype(jnp.bfloat16)

    def iteration(it):
        def flow_step(k):
            for other, out in ((True, theirs), (False, mine)):
                @pl.when(it == 0)
                def _():
                    fetch(k, other).wait()

                product(it, k, other, out)
                if other:
                    pair(it, k).start()

            @pl.when(k >= 1)
            def _():
                pass_on(it, k - 1)

        loop(half, flow_step)

        @pl.when(it == 0)
        def _():
            for copy in levels:
                copy.wait()
            for h in range(n):
                level[h:h + 1, :] = level_recv[h]

        pair(it, half - 1).wait_recv()
        total = mine[it, half - 1] + first_recv[it, half - 1] + own[...]
        for k in range(half - 1):
            row(it, k).wait_recv()
            total = total + second_recv[it, k].astype(jnp.float32)
        shifted = total.reshape(own_groups, hours, width)
        bound = limits_ref[pl.ds(me * own_groups, own_groups), :][:, None, :]
        clipped = jnp.minimum(jnp.maximum(shifted, -bound), bound)
        dual = (shifted - clipped).reshape(total.shape)
        all_dual[it, me] = dual.astype(jnp.bfloat16)
        own[...] = dual

        for k in range(quarter - 1):
            far_copy(it, k).start()
        mid_copy(it, 0).start()
        near_copy(it, 0).start()
        add_price(it, 0)

        def far_step(k):
            far_copy(it, k).wait_recv()
            mid_copy(it, k + 1).start()
            near_copy(it, k + 1).start()
            add_price(it, k + 1)

        def mid_step(k):
            mid_copy(it, k).wait_recv()
            near_copy(it, quarter + k).start()
            add_price(it, quarter + k)

        def near_step(k):
            near_copy(it, k).wait_recv()
            add_price(it, half + k)

        loop(quarter - 1, far_step)
        loop(quarter, mid_step)
        loop(half, near_step)
        update()
        loop(quarter - 1, lambda k: far_copy(it, k).wait_send())
        loop(quarter, lambda k: mid_copy(it, k).wait_send())

        def sent_all(k):
            near_copy(it, k).wait_send()
            pair(it, k).wait_send()

        loop(half, sent_all)
        loop(half - 1, lambda k: row(it, k).wait_send())

    loop(ITERS, iteration)

    for r in range(blocks):
        now = inj[r]
        for h in range(hours):
            inj_rows[h, :, r * width:(r + 1) * width] = now[h:h + 1]
    for g in range(own_groups):
        now = own[g * hours:(g + 1) * hours]
        for h in range(hours):
            dual_rows[h, :, g * width:(g + 1) * width] = now[h:h + 1]
    block = lax.div(bus_ref[...], width) - me * blocks
    kept = jnp.where((block >= 0) & (block < blocks), level[...], 0.0)
    for q in range(units // width):
        level_parts[:, q, :] = kept[:, q * width:(q + 1) * width]
    level_rows[...] = level_parts[...].astype(level_rows.dtype)
    inj_here = inj_out.at[:, pl.ds(pl.multiple_of(me * reach, reach), reach)]
    dual_here = dual_out.at[:, pl.ds(pl.multiple_of(me * span, span), span)]
    ends = []
    for k, other in enumerate(everyone):
        for part, (src, dst) in enumerate((
            (inj_rows.at[other], inj_here),
            (dual_rows.at[other], dual_here),
            (level_rows.at[other], level_last.at[k]),
        )):
            copy = remote(src, dst, end_send.at[part, k], end_recv.at[part, k], other)
            copy.start()
            ends.append(copy)
    inj_here[...] = inj_rows[me]
    dual_here[...] = dual_rows[me]
    for copy in ends:
        copy.wait()
    result = level_parts[me]
    for k in range(n - 1):
        result = result + level_last[k].astype(jnp.float32)
    level_out[...] = result


def admm(n, table, base_row, limits, unit_bus, gain, soc, tiles):
    half, quarter = n // 2, n // 4
    groups, depth, lines, width = tiles.shape
    hours = n
    blocks = base_row.shape[1] // n // width
    own_groups = groups // n
    units = soc.shape[1]
    chunk = (own_groups * hours, lines)
    grid = (blocks, hours, width)
    parts = (hours, units // width, width)
    dma = pltpu.SemaphoreType.DMA
    f32, bf16 = jnp.float32, jnp.bfloat16
    return pl.pallas_call(
        functools.partial(admm_kernel, n, 512 if units % 512 == 0 else units),
        out_shape=(
            jax.ShapeDtypeStruct(base_row.shape, f32),
            jax.ShapeDtypeStruct((1, groups * lines), f32),
            jax.ShapeDtypeStruct(parts[1:], f32),
        ),
        in_specs=[pl.BlockSpec(memory_space=pltpu.SMEM)] + [VM] * 6 + [pl.BlockSpec(memory_space=pl.ANY)],
        out_specs=(VM,) * 3,
        scratch_shapes=[
            pltpu.VMEM(tiles.shape, tiles.dtype),
            pltpu.VMEM((n, 1, blocks * width), bf16),
            pltpu.VMEM(grid, f32), pltpu.VMEM(grid, f32), pltpu.VMEM(grid, bf16), pltpu.VMEM(grid, f32),
            pltpu.VMEM((n, 1, units), f32),
            pltpu.VMEM((hours, units), f32),
            pltpu.VMEM((2 * depth, groups), jnp.int32),
            pltpu.SMEM((2 * depth, groups), jnp.int32),
            pltpu.VMEM((ITERS, half) + chunk, f32),
            pltpu.VMEM((ITERS, half) + chunk, f32),
            pltpu.VMEM((ITERS, half) + chunk, f32),
            pltpu.VMEM((ITERS, half - 1) + chunk, bf16),
            pltpu.VMEM((ITERS, half - 1) + chunk, bf16),
            pltpu.VMEM(chunk, f32),
            pltpu.VMEM((ITERS, n) + chunk, bf16),
            pltpu.VMEM((depth, groups + 1, hours, width), f32),
            pltpu.VMEM((hours, 1, blocks * width), f32),
            pltpu.VMEM((hours, 1, own_groups * lines), f32),
            pltpu.VMEM(parts, bf16),
            pltpu.VMEM(parts, f32),
            pltpu.VMEM((n - 1,) + parts[1:], bf16),
            dma((n,)), dma((1,)),
            dma((2, n - 1)), dma((2, n - 1)),
            dma((ITERS, half)), dma((ITERS, half)),
            dma((ITERS, half - 1)), dma((ITERS, half - 1)),
            dma((ITERS, quarter - 1)), dma((ITERS, quarter - 1)),
            dma((ITERS, quarter)), dma((ITERS, quarter)),
            dma((ITERS, half)), dma((ITERS, half)),
            dma((3, n - 1)), dma((3, n - 1)),
        ],
        compiler_params=pltpu.CompilerParams(collective_id=0, has_side_effects=True),
        name="admm",
    )(table, table, base_row, limits, unit_bus, gain, soc, tiles)


def finish_kernel(*refs):
    count = len(refs) // 2
    for src, dst in zip(refs[:count], refs[count:]):
        dst[...] = src[...]


def finish(*arrays):
    return pl.pallas_call(
        finish_kernel,
        out_shape=tuple(jax.ShapeDtypeStruct(a.shape, a.dtype) for a in arrays),
        in_specs=[VM] * len(arrays),
        out_specs=(VM,) * len(arrays),
        name="finish",
    )(*arrays)


def shards(base_injection, ptdf_tiles, tile_block, limits, stor_bus, stor_gain, soc_init):
    n = lax.axis_size("tm")
    groups, _, lines, width = ptdf_tiles.shape
    units = soc_init.shape[1]
    inj, dual, level = admm(
        n, tile_block.T, base_injection, limits.reshape(groups, lines), stor_bus.reshape(1, units),
        stor_gain.reshape(1, units), soc_init, ptdf_tiles,
    )
    inj, dual, level = finish(inj.reshape(-1, width), dual.reshape(-1, lines), level)
    return inj.reshape(1, -1), dual.reshape(1, -1), level.reshape(1, -1)


def solution(mesh):
    in_specs = (
        P(("scen", "tm"), None),
        P(None, "tm", None, None),
        P(None, "tm"),
        P(),
        P(),
        P(),
        P(("scen", "tm"), None),
    )
    out_specs = (P(("scen", "tm"), None), P(("scen", "tm"), None), P(("scen", "tm"), None))
    return jax.shard_map(shards, mesh=mesh, in_specs=in_specs, out_specs=out_specs, check_vma=False)
```

time: 111 us -> 70.5 us (0.64)
  Pallas kernels: 103 us -> 69.5 us
  local copies, waits for them, and re-layouts: 5.77 us -> 0 us
    pallas_call x6 -> x2, Pallas kernels: 103 us -> 69.5 us  [the longest x1 67.9 us: admm(): pl.pallas_call(functools.partial(admm_kernel, n, 512 if units % 512 == 0...]
    unnamed x4 -> x0, local copies, waits for them, and re-layouts: 5.77 us -> none
where the time goes in v1:
time: 70.5 us; the launch traced here: 70.2 us
  Pallas kernels  69.5 us (99%)
    pallas_call x1, Pallas kernels, admm(): pl.pallas_call(functools.partial(admm_kernel, n, 512 if units % 512 == 0...  67.9 us
    pallas_call x1, Pallas kernels, finish(): pl.pallas_call(finish_kernel, out_shape=tuple((jax.ShapeDtypeStruct(a.sha...  1.64 us

profile of v1, /device:TPU:0, one launch (start us, length us, event | category | flops | bytes accessed | tf_op | source)
XLA Modules:
  0.0 70.2 jit_solution(14531164006403286997)
XLA Ops:
  0.6 67.9 %admm.1 = (f32[1,36864]{1,0:T(1,128)}, f32[1,16384]{1,0:T(1,128)}, f32[16,128]{1,0:T(8,128)}) custom-call(s32[5,128]{1,0:T(8,128)} %bitcast.12, s32[5,128]{1,0:T(8,128)} %bitcast.13, bf16[1,36864]{1,0:T(2,128)(2,1)} %base_row_ref.1, f32[128,128]{1,0:T(8,128)} %bitcast.10, s32[1,2048]{1,0:T(1,128)} %bitcast.14, f32[1,2048]{1,0:T(1,128)} %bitcast.15, ...), custom_call_target="tpu_custom_call" | custom-call | tf_op jit(solution)/shard_map/admm/pallas_call | solution.py:338
  68.5 1.6 %finish.1 = (f32[288,128]{1,0:T(8,128)}, f32[128,128]{1,0:T(8,128)}, f32[16,128]{1,0:T(8,128)}) custom-call(f32[288,128]{1,0:T(8,128)} %bitcast.9, f32[128,128]{1,0:T(8,128)} %bitcast.11, f32[16,128]{1,0:T(8,128)} %get-tuple-element.11.refs_2_), custom_call_target="tpu_custom_call" | custom-call | tf_op jit(solution)/shard_map/finish/pallas_call | solution.py:389

commit v2 on v1

v2 whole, which is shorter than its diff:
```python
import functools

import jax
import jax.numpy as jnp
from jax import lax
from jax.experimental import pallas as pl
from jax.experimental.pallas import tpu as pltpu
from jax.sharding import PartitionSpec as P

ITERS = 2

step_size = 0.5
penalty = 4.0
ramp_weight = 0.5

VM = pl.BlockSpec(memory_space=pltpu.VMEM)
MESH = pl.DeviceIdType.MESH


def admm_kernel(
    n, unit_chunk, block_ref, block_rows_ref, base_row_ref, limits_ref, bus_ref, gain_ref, soc_ref, tiles_ref,
    ends_out, dual_out,
    held, rows, base, inj, sent, price, level_recv, level, pointers, table,
    theirs, mine, first_recv, first_sum, second_recv, own, all_dual, slots, moved, end_wide, end_rows,
    tile_sem, table_sem, start_send, start_recv, pair_send, pair_recv, row_send, row_recv,
    far_send, far_recv, mid_send, mid_recv, near_send, near_recv, end_send, end_recv,
):
    half, quarter = n // 2, n // 4
    groups, depth, _, width = held.shape
    blocks, hours = base.shape[:2]
    reach = blocks * width
    own_groups = groups // n
    units = level.shape[1]
    me = lax.axis_index("tm")
    core = lax.rem(me, 2)
    side = lax.rem(me // 2, 2)
    spot = me // 2
    far, lane = me // 4, lax.rem(me, 4)
    partner = me + 1 - 2 * core
    across = me + 2 - 4 * side
    everyone = [lax.rem(me + k, n) for k in range(1, n)]

    def remote(src, dst, send, recv, device):
        return pltpu.make_async_remote_copy(
            src_ref=src, dst_ref=dst, send_sem=send, recv_sem=recv,
            device_id={"tm": device}, device_id_type=MESH,
        )

    def owner(k, other):
        return lax.rem(spot + k + 1, half) * 2 + (1 - core if other else core)

    def fetch(k):
        place = pl.ds(lax.rem(spot + k + 1, half) * 2 * own_groups, 2 * own_groups)
        return pltpu.make_async_copy(tiles_ref.at[place], held.at[place], tile_sem.at[k])

    def chunk_at(pos):
        z = lax.rem(far + quarter - lax.rem(pos, quarter), quarter)
        y = lax.rem(side + lax.rem(pos // quarter, 2), 2)
        c = lax.rem(core + pos // half, 2)
        return z * 4 + y * 2 + c

    for k in range(half):
        fetch(k).start()

    barrier = pltpu.get_barrier_semaphore()
    for other in everyone:
        pl.semaphore_signal(barrier, inc=1, device_id={"tm": other}, device_id_type=MESH)

    group_pos = []
    for dim in (0, 1):
        g = lax.broadcasted_iota(jnp.int32, (groups, groups), dim)
        dev = lax.div(g, own_groups)
        turn = lax.rem(far + quarter - lax.div(dev, 4), quarter)
        other_side = lax.rem(lax.rem(lax.div(dev, 2), 2) + side, 2)
        other_core = lax.rem(lax.rem(dev, 2) + core, 2)
        pos = (other_core * half + other_side * quarter + turn) * own_groups + lax.rem(g, own_groups)
        group_pos.append(pos)
    down, along = group_pos
    numbers = lax.broadcasted_iota(jnp.int32, (groups, groups), 1)
    for k in range(depth):
        here = jnp.broadcast_to(block_rows_ref[k:k + 1, :], (groups, groups))
        there = here.T
        before = jnp.where((here == there) & (down < along), down + 1, 0)
        pointers[k:k + 1, :] = jnp.max(before, axis=0, keepdims=True)
        final = jnp.where(there == numbers, down + 1, 0)
        pointers[depth + k:depth + k + 1, :] = jnp.max(final, axis=0, keepdims=True)
    to_table = pltpu.make_async_copy(pointers, table, table_sem.at[0])
    to_table.start()
    own[...] = jnp.zeros_like(own)
    end_wide[...] = jnp.zeros_like(end_wide)
    for k in range(depth):
        slots[k, 0] = jnp.zeros((hours, width), jnp.float32)

    pl.semaphore_wait(barrier, n - 1)

    for other in everyone:
        remote(
            base_row_ref.at[:, pl.ds(pl.multiple_of(other * reach, reach), reach)], rows.at[me],
            start_send.at[0], start_recv.at[0], other,
        ).start()
    for other in everyone:
        remote(soc_ref, level_recv.at[me], start_send.at[1], start_recv.at[1], other).start()
    others = pl.ds(0, n - 1)
    starts = remote(rows.at[others], rows.at[others], start_send.at[0], start_recv.at[0], partner)
    levels = remote(level_recv.at[others], level_recv.at[others], start_send.at[1], start_recv.at[1], partner)
    rows[me] = base_row_ref[:, pl.ds(pl.multiple_of(me * reach, reach), reach)]
    level_recv[me] = soc_ref[...]
    to_table.wait()
    starts.wait()
    for h in range(n):
        row = rows[h].astype(jnp.float32)
        for b in range(blocks):
            base[b, h:h + 1, :] = row[:, b * width:(b + 1) * width]
    inj[...] = base[...]
    sent[...] = base[...].astype(sent.dtype)

    def product(it, k, other, out):
        first = owner(k, other) * own_groups
        for g in range(own_groups):
            picked = jnp.concatenate([sent[block_ref[t, first + g]] for t in range(depth)], axis=1)
            wide = jnp.concatenate([held[first + g, t] for t in range(depth)], axis=1)
            out[it, k, g * hours:(g + 1) * hours] = lax.dot_general(
                picked, wide, (((1,), (1,)), ((), ())), preferred_element_type=jnp.float32
            )

    def pair(it, k):
        return remote(
            theirs.at[it, k], first_recv.at[it, k], pair_send.at[0], pair_recv.at[it, k], partner
        )

    def row(it, k):
        return remote(
            first_sum.at[it, k], second_recv.at[it, k], row_send.at[0], row_recv.at[it],
            lax.rem(spot + k + 1, half) * 2 + core,
        )

    def far_copy(it, k):
        chunk = all_dual.at[it, me]
        device = lax.rem(far + k + 1, quarter) * 4 + lane
        return remote(chunk, chunk, far_send.at[0], far_recv.at[it, k], device)

    def mid_copy(it, k):
        chunk = all_dual.at[it, chunk_at(k)]
        return remote(chunk, chunk, mid_send.at[0], mid_recv.at[it, k], across)

    def near_copy(it, k):
        chunk = all_dual.at[it, chunk_at(k)]
        return remote(chunk, chunk, near_send.at[0], near_recv.at[it, k], partner)

    def pass_on(it, k):
        pair(it, k).wait_recv()
        first_sum[it, k] = (mine[it, k] + first_recv[it, k]).astype(jnp.bfloat16)
        row(it, k).start()

    def add_price(it, pos):
        chunk = chunk_at(pos)
        for g in range(own_groups):
            group = chunk * own_groups + g
            place = pos * own_groups + g + 1
            wide = jnp.concatenate([held[group, k] for k in range(depth)], axis=1)
            part = jnp.dot(
                all_dual[it, chunk, g * hours:(g + 1) * hours], wide, preferred_element_type=jnp.float32
            )
            for k in range(depth):
                slots[k, place] = slots[k, table[k, group]] + part[:, k * width:(k + 1) * width]

    def loop(count, body):
        def step(k, carry):
            body(k)
            return carry

        lax.fori_loop(0, count, step, 0)

    def unit_part(start):
        part = pl.ds(start, unit_chunk)
        bus = bus_ref[:, part]
        block = jnp.broadcast_to(lax.div(bus, width) - me * blocks, (hours, unit_chunk))
        spots = lax.broadcasted_iota(jnp.int32, (width, unit_chunk), 0)
        chosen = jnp.where(spots == lax.rem(bus, width), 1.0, 0.0).astype(jnp.bfloat16)
        return part, block, chosen

    def move_charges():
        total = jnp.zeros((blocks * hours, width), jnp.float32)
        for start in range(0, units, unit_chunk):
            part, block, chosen = unit_part(start)
            now = level[:, part]
            charge = now - pltpu.roll(now, 1, 0)
            spread = jnp.concatenate(
                [jnp.where(block == r, charge, 0.0).astype(jnp.bfloat16) for r in range(blocks)], axis=0
            )
            total = total + lax.dot_general(
                spread, chosen, (((1,), (1,)), ((), ())), preferred_element_type=jnp.float32
            )
        moved[...] = total

    def update():
        for r in range(blocks):
            total = slots[0, table[depth, r]]
            for k in range(1, depth):
                total = total + slots[k, table[depth + k, r]]
            price[r] = total
        flat = price[...].astype(jnp.bfloat16).reshape(blocks * hours, width)
        for start in range(0, units, unit_chunk):
            part, block, chosen = unit_part(start)
            now = level[:, part]
            found = jnp.dot(flat, chosen, preferred_element_type=jnp.float32)
            store_price = jnp.zeros_like(now)
            for r in range(blocks):
                store_price = store_price + jnp.where(block == r, found[r * hours:(r + 1) * hours], 0.0)
            level[:, part] = 0.5 * (now + pltpu.roll(now, 1, 0)) - gain_ref[:, part] * store_price
        for r in range(blocks):
            now = inj[r]
            ramp = 2.0 * now - pltpu.roll(now, 1, 0) - pltpu.roll(now, hours - 1, 0)
            updated = now - step_size * ((now - base[r]) + penalty * price[r] + ramp_weight * ramp)
            updated = updated - step_size * moved[r * hours:(r + 1) * hours]
            inj[r] = updated
            sent[r] = updated.astype(jnp.bfloat16)

    def iteration(it):
        def flow_step(k):
            @pl.when(it == 0)
            def _():
                fetch(k).wait()

            product(it, k, True, theirs)
            product(it, k, False, mine)
            pair(it, k).start()

            @pl.when(k >= 1)
            def _():
                pass_on(it, k - 1)

        loop(half, flow_step)

        @pl.when(it == 0)
        def _():
            levels.wait()
            for h in range(n):
                level[h:h + 1, :] = level_recv[h]

        pair(it, half - 1).wait_recv()
        total = mine[it, half - 1] + first_recv[it, half - 1] + own[...]
        remote(
            first_sum.at[it], second_recv.at[it], row_send.at[0], row_recv.at[it], partner
        ).wait_recv()
        for k in range(half - 1):
            total = total + second_recv[it, k].astype(jnp.float32)
        shifted = total.reshape(own_groups, hours, width)
        bound = limits_ref[pl.ds(me * own_groups, own_groups), :][:, None, :]
        clipped = jnp.minimum(jnp.maximum(shifted, -bound), bound)
        dual = (shifted - clipped).reshape(total.shape)
        all_dual[it, me] = dual.astype(jnp.bfloat16)
        own[...] = dual

        for k in range(quarter - 1):
            far_copy(it, k).start()
        mid_copy(it, 0).start()
        near_copy(it, 0).start()
        add_price(it, 0)
        move_charges()

        def far_step(k):
            far_copy(it, k).wait_recv()
            mid_copy(it, k + 1).start()
            near_copy(it, k + 1).start()
            add_price(it, k + 1)

        def mid_step(k):
            mid_copy(it, k).wait_recv()
            near_copy(it, quarter + k).start()
            add_price(it, quarter + k)

        def near_step(k):
            near_copy(it, k).wait_recv()
            add_price(it, half + k)

        loop(quarter - 1, far_step)
        loop(quarter, mid_step)
        loop(half, near_step)
        update()
        for buffer, sem, count in (
            (all_dual, far_send, quarter - 1), (all_dual, mid_send, quarter), (all_dual, near_send, half),
            (theirs, pair_send, half), (first_sum, row_send, half - 1),
        ):
            whole = buffer.at[it, pl.ds(0, count)]
            remote(whole, whole, sem.at[0], row_recv.at[it], partner).wait_send()

    loop(ITERS, iteration)

    for r in range(blocks):
        end_wide[:, r, :] = inj[r]
    block = lax.div(bus_ref[...], width) - me * blocks
    kept = jnp.where((block >= 0) & (block < blocks), level[...], 0.0)
    for q in range(units // width):
        end_wide[:, blocks + q, :] = kept[:, q * width:(q + 1) * width]
    end_rows[...] = end_wide[...].astype(end_rows.dtype)
    for other in everyone:
        remote(end_rows.at[other], ends_out.at[me], end_send.at[0], end_recv.at[0], other).start()
    ends_out[me] = end_rows[me]
    hour = lax.broadcasted_iota(jnp.int32, (own_groups, hours, width), 1)
    for c in range(n):
        dual = all_dual[ITERS - 1, c].astype(jnp.float32).reshape(own_groups, hours, width)
        dual_out[c * own_groups:(c + 1) * own_groups, :] = jnp.sum(jnp.where(hour == me, dual, 0.0), axis=1)
    remote(end_rows.at[others], ends_out.at[others], end_send.at[0], end_recv.at[0], partner).wait()


def admm(n, table, base_row, limits, unit_bus, gain, soc, tiles):
    half, quarter = n // 2, n // 4
    groups, depth, lines, width = tiles.shape
    hours = n
    blocks = base_row.shape[1] // n // width
    own_groups = groups // n
    units = soc.shape[1]
    chunk = (own_groups * hours, lines)
    grid = (blocks, hours, width)
    ends = (hours, pl.cdiv(blocks + units // width, 8) * 8, width)
    dma = pltpu.SemaphoreType.DMA
    f32, bf16 = jnp.float32, jnp.bfloat16
    return pl.pallas_call(
        functools.partial(admm_kernel, n, 512 if units % 512 == 0 else units),
        out_shape=(
            jax.ShapeDtypeStruct(ends, bf16),
            jax.ShapeDtypeStruct((groups, lines), f32),
        ),
        in_specs=[pl.BlockSpec(memory_space=pltpu.SMEM)] + [VM] * 6 + [pl.BlockSpec(memory_space=pl.ANY)],
        out_specs=(VM,) * 2,
        scratch_shapes=[
            pltpu.VMEM(tiles.shape, tiles.dtype),
            pltpu.VMEM((n, 1, blocks * width), bf16),
            pltpu.VMEM(grid, f32), pltpu.VMEM(grid, f32), pltpu.VMEM(grid, bf16), pltpu.VMEM(grid, f32),
            pltpu.VMEM((n, 1, units), f32),
            pltpu.VMEM((hours, units), f32),
            pltpu.VMEM((2 * depth, groups), jnp.int32),
            pltpu.SMEM((2 * depth, groups), jnp.int32),
            pltpu.VMEM((ITERS, half) + chunk, f32),
            pltpu.VMEM((ITERS, half) + chunk, f32),
            pltpu.VMEM((ITERS, half) + chunk, f32),
            pltpu.VMEM((ITERS, half - 1) + chunk, bf16),
            pltpu.VMEM((ITERS, half - 1) + chunk, bf16),
            pltpu.VMEM(chunk, f32),
            pltpu.VMEM((ITERS, n) + chunk, bf16),
            pltpu.VMEM((depth, groups + 1, hours, width), f32),
            pltpu.VMEM((blocks * hours, width), f32),
            pltpu.VMEM(ends, f32),
            pltpu.VMEM(ends, bf16),
            dma((half,)), dma((1,)), dma((2,)), dma((2,)),
            dma((1,)), dma((ITERS, half)),
            dma((1,)), dma((ITERS,)),
            dma((1,)), dma((ITERS, quarter - 1)),
            dma((1,)), dma((ITERS, quarter)),
            dma((1,)), dma((ITERS, half)),
            dma((1,)), dma((1,)),
        ],
        compiler_params=pltpu.CompilerParams(collective_id=0, has_side_effects=True),
        name="admm",
    )(table, table, base_row, limits, unit_bus, gain, soc, tiles)


def finish_kernel(ends_ref, dual_ref, inj_out, dual_out, level_out):
    count = ends_ref.shape[0]
    blocks = inj_out.shape[0] // count
    own = level_out.shape[0]
    total = jnp.zeros(level_out.shape, jnp.float32)
    for d in range(count):
        part = ends_ref[d].astype(jnp.float32)
        inj_out[d * blocks:(d + 1) * blocks, :] = part[:blocks]
        total = total + part[blocks:blocks + own]
    level_out[...] = total
    dual_out[...] = dual_ref[...]


def finish(ends, dual, buses, units):
    width = ends.shape[2]
    f32 = jnp.float32
    return pl.pallas_call(
        finish_kernel,
        out_shape=(
            jax.ShapeDtypeStruct((buses // width, width), f32),
            jax.ShapeDtypeStruct(dual.shape, f32),
            jax.ShapeDtypeStruct((units // width, width), f32),
        ),
        in_specs=[VM] * 2,
        out_specs=(VM,) * 3,
        name="finish",
    )(ends, dual)


def shards(base_injection, ptdf_tiles, tile_block, limits, stor_bus, stor_gain, soc_init):
    n = lax.axis_size("tm")
    groups, _, lines, _ = ptdf_tiles.shape
    units = soc_init.shape[1]
    ends, dual = admm(
        n, tile_block.T, base_injection, limits.reshape(groups, lines), stor_bus.reshape(1, units),
        stor_gain.reshape(1, units), soc_init, ptdf_tiles,
    )
    inj, dual, level = finish(ends, dual, base_injection.shape[1], units)
    return inj.reshape(1, -1), dual.reshape(1, -1), level.reshape(1, -1)


def solution(mesh):
    in_specs = (
        P(("scen", "tm"), None),
        P(None, "tm", None, None),
        P(None, "tm"),
        P(),
        P(),
        P(),
        P(("scen", "tm"), None),
    )
    out_specs = (P(("scen", "tm"), None), P(("scen", "tm"), None), P(("scen", "tm"), None))
    return jax.shard_map(shards, mesh=mesh, in_specs=in_specs, out_specs=out_specs, check_vma=False)
```

time: 70.5 us -> 67.1 us (0.952)
  Pallas kernels: 69.5 us -> 66.3 us
    pallas_call x1, Pallas kernels: 67.9 us -> 64.7 us  [admm(): pl.pallas_call(functools.partial(admm_kernel, n, 512 if units % 512 == 0...]
where the time goes in v2:
time: 67.1 us; the launch traced here: 67 us
  Pallas kernels  66.3 us (99%)
    pallas_call x1, Pallas kernels, admm(): pl.pallas_call(functools.partial(admm_kernel, n, 512 if units % 512 == 0...  64.7 us
    pallas_call x1, Pallas kernels, finish(): pl.pallas_call(finish_kernel, out_shape=(jax.ShapeDtypeStruct((buses // w...  1.61 us

profile of v2, /device:TPU:0, one launch (start us, length us, event | category | flops | bytes accessed | tf_op | source)
XLA Modules:
  0.0 67.0 jit_solution(1883841880360815433)
XLA Ops:
  0.6 64.7 %admm.1 = (bf16[16,40,128]{2,1,0:T(8,128)(2,1)}, f32[128,128]{1,0:T(8,128)}) custom-call(s32[5,128]{1,0:T(8,128)} %bitcast.8, s32[5,128]{1,0:T(8,128)} %bitcast.9, bf16[1,36864]{1,0:T(2,128)(2,1)} %base_row_ref.1, f32[128,128]{1,0:T(8,128)} %bitcast.7, s32[1,2048]{1,0:T(1,128)} %bitcast.10, f32[1,2048]{1,0:T(1,128)} %bitcast.11, f32[1,2048]{1,0:T(1,128)} %soc_ref.1, ...), custom_call_target="tpu_custom_call" | custom-call | tf_op jit(solution)/shard_map/admm/pallas_call | solution.py:319
  65.4 1.6 %finish.1 = (f32[288,128]{1,0:T(8,128)}, f32[128,128]{1,0:T(8,128)}, f32[16,128]{1,0:T(8,128)}) custom-call(bf16[16,40,128]{2,1,0:T(8,128)(2,1)} %get-tuple-element.8.ends_ref, f32[128,128]{1,0:T(8,128)} %get-tuple-element.9.dual_ref), custom_call_target="tpu_custom_call" | custom-call | tf_op jit(solution)/shard_map/finish/pallas_call | solution.py:375

commit v3 on v2

--- a/solution.py
+++ b/solution.py
@@ -271,12 +271,14 @@
             add_price(it, quarter + k)
 
         def near_step(k):
-            near_copy(it, k).wait_recv()
-            add_price(it, half + k)
+            for j in range(2):
+                near_copy(it, 2 * k + j).wait_recv()
+            for j in range(2):
+                add_price(it, half + 2 * k + j)
 
         loop(quarter - 1, far_step)
         loop(quarter, mid_step)
-        loop(half, near_step)
+        loop(half // 2, near_step)
         update()
         for buffer, sem, count in (
             (all_dual, far_send, quarter - 1), (all_dual, mid_send, quarter), (all_dual, near_send, half),

time: 67.1 us -> 66.3 us (0.988)
  Pallas kernels: 66.3 us -> 65.5 us
    pallas_call x1, Pallas kernels: 64.7 us -> 63.9 us  [admm(): pl.pallas_call(functools.partial(admm_kernel, n, 512 if units % 512 == 0...]
where the time goes in v3:
time: 66.3 us; the launch traced here: 66.1 us
  Pallas kernels  65.5 us (99%)
    pallas_call x1, Pallas kernels, admm(): pl.pallas_call(functools.partial(admm_kernel, n, 512 if units % 512 == 0...  63.9 us
    pallas_call x1, Pallas kernels, finish(): pl.pallas_call(finish_kernel, out_shape=(jax.ShapeDtypeStruct((buses // w...  1.61 us

profile of v3, /device:TPU:0, one launch (start us, length us, event | category | flops | bytes accessed | tf_op | source)
XLA Modules:
  0.0 66.1 jit_solution(13830905632296581394)
XLA Ops:
  0.6 63.9 %admm.1 = (bf16[16,40,128]{2,1,0:T(8,128)(2,1)}, f32[128,128]{1,0:T(8,128)}) custom-call(s32[5,128]{1,0:T(8,128)} %bitcast.8, s32[5,128]{1,0:T(8,128)} %bitcast.9, bf16[1,36864]{1,0:T(2,128)(2,1)} %base_row_ref.1, f32[128,128]{1,0:T(8,128)} %bitcast.7, s32[1,2048]{1,0:T(1,128)} %bitcast.10, f32[1,2048]{1,0:T(1,128)} %bitcast.11, f32[1,2048]{1,0:T(1,128)} %soc_ref.1, ...), custom_call_target="tpu_custom_call" | custom-call | tf_op jit(solution)/shard_map/admm/pallas_call | solution.py:321
  64.5 1.6 %finish.1 = (f32[288,128]{1,0:T(8,128)}, f32[128,128]{1,0:T(8,128)}, f32[16,128]{1,0:T(8,128)}) custom-call(bf16[16,40,128]{2,1,0:T(8,128)(2,1)} %get-tuple-element.8.ends_ref, f32[128,128]{1,0:T(8,128)} %get-tuple-element.9.dual_ref), custom_call_target="tpu_custom_call" | custom-call | tf_op jit(solution)/shard_map/finish/pallas_call | solution.py:377
